TPU v7x, 32 devices: a whole 2x2x4 slice. The times are simulated.
32 devices in a mesh: groups: 2 (over x), seq: 16 (over z, y, core).
Axes of the slice: x: 2, y: 2, z: 4, core: 2. Of those that a mesh axis runs over, the one named last changes fastest.
Arguments:
- atoms: bfloat16 [2, 8192, 128], P('groups', 'seq'), parts along dimension 0, may hold values from -6 to 6
- s_cond: bfloat16 [2048, 768], P(('groups', 'seq')), parts along dimension 0, may hold values from -6 to 6
- token_start: int32 [2048], P(('groups', 'seq')), parts along dimension 0, may hold values from 0 to 8191, as said below
- token_len: int32 [2048], P(('groups', 'seq')), parts along dimension 0, may hold values from 1 to 12, as said below
- atom_mask: int32 [16384], P(('groups', 'seq')), parts along dimension 0, may hold values 0 or 1
- atom_bias: float32 [8, 8192, 128], P('groups', 'seq'), parts along dimension 0, may hold values from -4 to 250
- pair_bias: bfloat16 [32, 1024, 1024], P('groups', 'seq'), parts along dimension 0, may hold values from -4 to 250
- atom_proj: bfloat16 [6, 4, 128, 128], replicated, may hold values from -0.5 to 0.5
- atom_up: bfloat16 [6, 2, 128, 256], replicated, may hold values from -0.5 to 0.5
- atom_down: bfloat16 [6, 256, 128], replicated, may hold values from -0.375 to 0.375
- atom_gains: float32 [6, 2, 128], replicated, may hold values from 0.5 to 1.5
- to_token: bfloat16 [128, 768], replicated, may hold values from -0.5 to 0.5
- token_proj: bfloat16 [4, 768, 768], replicated, may hold values from -0.21875 to 0.21875
- token_gain: float32 [768], replicated, may hold values from 0.5 to 2
- to_atom: bfloat16 [768, 128], replicated, may hold values from -0.21875 to 0.21875
Outputs:
- atoms_out: bfloat16 [2, 8192, 128], P('groups', 'seq'), parts along dimension 0
There are 2 independent parts, one for each index of `groups`. A program takes and returns all parts, laid end to end along the dimension named above; an argument that names none is the same for every part. Nothing has to cross between parts.
Inputs may be any that keep to these rules, and one draw needn't show every extreme that they name: Token t lies in block d = t // 64; its atoms token_start[t] .. token_start[t] + token_len[t] - 1 lie within atoms (d - 1) * 512 .. (d + 2) * 512 - 1 and within the complex. Ranges of the tokens of one block are disjoint and rise with t; ranges of different blocks may share atoms; atoms may belong to no token. `token_len`: every block of 64 tokens has a token of exactly 12 atoms.
All inputs are finite; a program needn't handle non-finite values. No bound on the sum of `atom_mask` on one device may be relied on, other than what follows from the above.
Results may differ from a plain program's by a relative error of at most 0.024.
Values may be sent and summed in bfloat16 or wider, within the bound.
A program may use at most 128 MiB of HBM per device.

v0:
```python
import functools

import jax
import jax.numpy as jnp
from jax import lax
from jax.experimental import pallas as pl
from jax.experimental.pallas import tpu as pltpu
from jax.sharding import PartitionSpec as P

HT = 16
HA = 4
WQ = 32
WK = 128
ENC_LAYERS = 3
DEC_LAYERS = 3
RIM = (WK - WQ) // 2
GROUP = 4
CHUNK = 256
LANES = 128

epsilon = 1e-05
masked = -1000000000.0
MESH = pl.DeviceIdType.MESH
F32 = jnp.float32
BF16 = jnp.bfloat16


def layer_norm(values, gain_vec):
    average = jnp.mean(values, axis=-1, keepdims=True)
    centred = values - average
    spread = jnp.mean(centred * centred, axis=-1, keepdims=True)
    return centred * lax.rsqrt(spread + epsilon) * gain_vec


def mm(left, right):
    return jnp.dot(left, right, preferred_element_type=F32)


def mm_nt(left, right):
    return lax.dot_general(left, right, (((1,), (1,)), ((), ())), preferred_element_type=F32)


def head_mask(rows, row_size, cols, col_size):
    row_head = lax.broadcasted_iota(jnp.int32, (rows, cols), 0) // row_size
    col_head = lax.broadcasted_iota(jnp.int32, (rows, cols), 1) // col_size
    return row_head == col_head


def kernel(
    count,
    atoms_ref,
    s_cond_ref,
    range_ref,
    mask_ref,
    bias_hbm,
    pair_hbm,
    proj_ref,
    up_ref,
    down_ref,
    gains_ref,
    to_token_ref,
    token_proj_hbm,
    token_gain_ref,
    to_atom_ref,
    out_ref,
    x_ref,
    kv_ref,
    q_ref,
    mix_ref,
    bias_ref,
    pair_ref,
    tp_ref,
    mex_ref,
    wmask_ref,
    rngx_ref,
    encx_ref,
    rowsx_ref,
    uall_ref,
    feat_ref,
    qbd_ref,
    acc_ref,
    max_ref,
    sum_ref,
    load_sem,
    halo_send,
    halo_recv,
    side_send,
    side_recv,
    u_send,
    u_recv,
):
    me = lax.axis_index("seq")
    core = lax.rem(me, 2)
    row_y = lax.rem(me // 2, 2)
    row_z = me // 4
    depth = count // 4
    has_left = me > 0
    has_right = me < count - 1
    atoms_dev = atoms_ref.shape[1]
    channels = atoms_ref.shape[2]
    tokens_dev, width = s_cond_ref.shape
    windows = atoms_dev // WQ
    head_size = channels // HA
    token_head = width // HT
    core_peer = me + 1 - 2 * core
    y_peer = me + 2 - 4 * row_y

    bias_load = pltpu.make_async_copy(bias_hbm, bias_ref, load_sem.at[0])
    tp_load = pltpu.make_async_copy(token_proj_hbm, tp_ref, load_sem.at[1])
    pair_load = pltpu.make_async_copy(pair_hbm, pair_ref, load_sem.at[2])
    bias_load.start()

    barrier = pltpu.get_barrier_semaphore()

    def greet(target):
        pl.semaphore_signal(barrier, inc=1, device_id={"seq": target}, device_id_type=MESH)

    greet(y_peer)
    pl.when(has_left)(lambda: greet(me - 1))
    pl.when(has_right)(lambda: greet(me + 1))
    pl.when(row_z > 0)(lambda: greet(me - 4))
    pl.when(row_z < depth - 1)(lambda: greet(me + 4))
    tp_load.start()
    pair_load.start()

    x_ref[...] = atoms_ref[0].astype(F32)
    mex_ref[1] = mask_ref[...]
    rngx_ref[1] = range_ref[...]

    def clear(slot, edge):
        for ref in (mex_ref, rngx_ref, encx_ref, rowsx_ref):
            ref[slot] = jnp.zeros(ref.shape[1:], ref.dtype)
        for layer in range(ENC_LAYERS + DEC_LAYERS):
            for kind in range(2):
                kv_ref[layer, kind, edge : edge + RIM] = jnp.zeros((RIM, channels), BF16)

    pl.when(jnp.logical_not(has_left))(lambda: clear(0, 0))
    pl.when(jnp.logical_not(has_right))(lambda: clear(2, RIM + atoms_dev))

    peers = 1 + sum(
        jnp.where(there, 1, 0)
        for there in (has_left, has_right, row_z > 0, row_z < depth - 1)
    )
    pl.semaphore_wait(barrier, peers)

    def side_copies(src_left, dst_left, src_right, dst_right, send, recv):
        to_left = pltpu.make_async_remote_copy(
            src_left, dst_left, send(0), recv(0), device_id={"seq": me - 1}, device_id_type=MESH
        )
        to_right = pltpu.make_async_remote_copy(
            src_right, dst_right, send(1), recv(1), device_id={"seq": me + 1}, device_id_type=MESH
        )
        return to_left, to_right

    def start_sides(copies):
        pl.when(has_left)(lambda: copies[0].start())
        pl.when(has_right)(lambda: copies[1].start())

    def receive_sides(copies):
        pl.when(has_right)(lambda: copies[0].wait_recv())
        pl.when(has_left)(lambda: copies[1].wait_recv())

    def sent_sides(copies):
        pl.when(has_left)(lambda: copies[0].wait_send())
        pl.when(has_right)(lambda: copies[1].wait_send())

    def block_sides(src, ref, slot):
        return side_copies(
            src,
            ref.at[2],
            src,
            ref.at[0],
            lambda side: side_send.at[slot, side],
            lambda side: side_recv.at[slot, side],
        )

    def halo_sides(layer):
        return side_copies(
            kv_ref.at[layer, :, pl.ds(RIM, RIM)],
            kv_ref.at[layer, :, pl.ds(RIM + atoms_dev, RIM)],
            kv_ref.at[layer, :, pl.ds(atoms_dev, RIM)],
            kv_ref.at[layer, :, pl.ds(0, RIM)],
            lambda side: halo_send.at[layer, side],
            lambda side: halo_recv.at[layer, side],
        )

    mask_sides = block_sides(mask_ref, mex_ref, 0)
    range_sides = block_sides(range_ref, rngx_ref, 1)
    start_sides(mask_sides)
    start_sides(range_sides)

    def window_masks():
        receive_sides(mask_sides)
        rows = atoms_dev // LANES

        def mask_row(index):
            return mex_ref[index // rows, index % rows : index % rows + 1, :]

        for window in range(windows):
            first = atoms_dev + window * WQ - RIM
            row, offset = first // LANES, first % LANES
            line = mask_row(row)
            if offset:
                line = jnp.concatenate(
                    [line[:, offset:], mask_row(row + 1)[:, :offset]], axis=1
                )
            wmask_ref[window] = jnp.where(line == 1, 0.0, masked).astype(F32)

    atom_heads = head_mask(HA * WQ, WQ, channels, head_size)

    def attend(layer, window):
        first = pl.multiple_of(window * WQ, WQ)
        query = q_ref[pl.ds(first, WQ), :]
        tall = jnp.where(
            atom_heads, jnp.concatenate([query] * HA, axis=0), jnp.zeros((), BF16)
        )
        keys = kv_ref[layer, 0, pl.ds(first, WK), :]
        values = kv_ref[layer, 1, pl.ds(first, WK), :]
        bias = bias_ref[:, pl.ds(first, WQ), :].reshape(HA * WQ, WK)
        logits = mm_nt(tall, keys) * head_size ** (-0.5) + bias + wmask_ref[window]
        weights = jnp.exp(logits - jnp.max(logits, axis=-1, keepdims=True))
        total = jnp.sum(weights, axis=-1, keepdims=True)
        mixed = mm(weights.astype(BF16), values) * (1.0 / total)
        mixed = jnp.where(atom_heads, mixed, 0.0)
        joined = mixed[0:WQ]
        for head in range(1, HA):
            joined = joined + mixed[head * WQ : (head + 1) * WQ]
        mix_ref[pl.ds(first, WQ), :] = joined.astype(BF16)

    def atom_block(layer):
        copies = halo_sides(layer)
        gain = gains_ref[layer]
        for base in range(0, atoms_dev, CHUNK):
            normed = layer_norm(x_ref[base : base + CHUNK], gain[0:1]).astype(BF16)
            for kind in range(2):
                kv_ref[layer, kind, RIM + base : RIM + base + CHUNK] = mm(
                    normed, proj_ref[layer, kind + 1]
                ).astype(BF16)
            q_ref[base : base + CHUNK] = mm(normed, proj_ref[layer, 0]).astype(BF16)
        start_sides(copies)

        def inner(step, carry):
            for part in range(GROUP):
                attend(layer, 2 + step * GROUP + part)
            return carry

        lax.fori_loop(0, (windows - 4) // GROUP, inner, 0)
        receive_sides(copies)
        for window in (0, 1, windows - 2, windows - 1):
            attend(layer, window)
        for base in range(0, atoms_dev, CHUNK):
            stream = x_ref[base : base + CHUNK] + mm(
                mix_ref[base : base + CHUNK], proj_ref[layer, 3]
            )
            second = layer_norm(stream, gain[1:2]).astype(BF16)
            gated = jax.nn.silu(mm(second, up_ref[layer, 0]))
            hidden = (gated * mm(second, up_ref[layer, 1])).astype(BF16)
            x_ref[base : base + CHUNK] = stream + mm(hidden, down_ref[layer])

    def loop_blocks(low, high):
        def step(layer, carry):
            atom_block(layer)
            return carry

        lax.fori_loop(low, high, step, 0)

    window_masks()
    bias_load.wait()
    loop_blocks(0, ENC_LAYERS)

    encx_ref[1] = x_ref[...].astype(BF16)
    enc_sides = block_sides(encx_ref.at[1], encx_ref, 2)
    start_sides(enc_sides)
    receive_sides(range_sides)
    eye = head_mask(tokens_dev, 1, tokens_dev, 1)

    def column(line):
        return jnp.sum(jnp.where(eye, line.astype(F32), 0.0), axis=1, keepdims=True)

    start_col = column(rngx_ref[1, 0:1, 0:tokens_dev])
    end_col = column(rngx_ref[1, 1:2, 0:tokens_dev])

    def pooled(block):
        projected = jnp.maximum(mm(encx_ref[block], to_token_ref[...]), 0.0).astype(BF16)
        place = (me + block - 1) * atoms_dev + lax.broadcasted_iota(
            jnp.int32, (tokens_dev, atoms_dev), 1
        )
        place = place.astype(F32)
        member = jnp.where((place >= start_col) & (place < end_col), 1.0, 0.0).astype(BF16)
        return mm(member, projected)

    totals = pooled(1)
    receive_sides(enc_sides)
    totals = totals + pooled(0) + pooled(2)
    features = totals / (end_col - start_col) + s_cond_ref[...].astype(F32)
    feat_ref[...] = features
    uall_ref[me] = layer_norm(features, token_gain_ref[...]).astype(BF16)

    def at(z, y, c):
        return (z * 2 + y) * 2 + c

    def u_copy(index, target, kind):
        return pltpu.make_async_remote_copy(
            uall_ref.at[index],
            uall_ref.at[index],
            u_send.at[index, kind],
            u_recv.at[index],
            device_id={"seq": target},
            device_id_type=MESH,
        )

    def u_arrived(index):
        u_copy(index, core_peer, 3).wait_recv()

    def own_sends(act):
        pl.when(row_z > 0)(lambda: act(u_copy(me, me - 4, 0)))
        pl.when(row_z < depth - 1)(lambda: act(u_copy(me, me + 4, 1)))
        act(u_copy(me, y_peer, 2))
        act(u_copy(me, core_peer, 3))

    def relay_sends(z, act):
        index = at(z, row_y, core)
        pl.when((z < row_z) & (row_z < depth - 1))(lambda: act(u_copy(index, me + 4, 1)))
        pl.when((z > row_z) & (row_z > 0))(lambda: act(u_copy(index, me - 4, 0)))
        act(u_copy(index, y_peer, 2))
        act(u_copy(index, core_peer, 3))

    def relay(z):
        u_arrived(at(z, row_y, core))
        relay_sends(z, lambda copy: copy.start())

    own_sends(lambda copy: copy.start())

    tp_load.wait()
    half = HT // 2
    half_width = width // 2
    token_heads = head_mask(half * tokens_dev, tokens_dev, half_width, token_head)
    for part in range(2):
        cols = slice(part * half_width, (part + 1) * half_width)
        query = mm(uall_ref[me], tp_ref[0, :, cols]).astype(BF16)
        qbd_ref[part] = jnp.where(
            token_heads, jnp.concatenate([query] * half, axis=0), jnp.zeros((), BF16)
        )
    max_ref[...] = jnp.full_like(max_ref, -1e30)
    sum_ref[...] = jnp.zeros_like(sum_ref)
    acc_ref[...] = jnp.zeros_like(acc_ref)
    pair_load.wait()
    span = 4 * tokens_dev

    def token_block(z):
        rows = uall_ref[pl.ds(4 * z, 4)].reshape(span, width)
        first = pl.multiple_of(z * span, span)
        for part in range(2):
            cols = slice(part * half_width, (part + 1) * half_width)
            keys = mm(rows, tp_ref[1, :, cols]).astype(BF16)
            values = mm(rows, tp_ref[2, :, cols]).astype(BF16)
            bias = pair_ref[part * half : (part + 1) * half, :, pl.ds(first, span)]
            bias = bias.reshape(half * tokens_dev, span).astype(F32)
            logits = mm_nt(qbd_ref[part], keys) * token_head ** (-0.5) + bias
            before = max_ref[part][:, 0:1]
            now = jnp.maximum(before, jnp.max(logits, axis=-1, keepdims=True))
            weights = jnp.exp(logits - now)
            shrink = jnp.exp(before - now)
            total = sum_ref[part][:, 0:1] * shrink + jnp.sum(weights, axis=-1, keepdims=True)
            acc_ref[part] = acc_ref[part] * shrink + mm(weights.astype(BF16), values)
            max_ref[part] = jnp.broadcast_to(now, max_ref.shape[1:])
            sum_ref[part] = jnp.broadcast_to(total, sum_ref.shape[1:])

    def block_done(z):
        across = at(z, 1 - row_y, core)
        u_arrived(across)
        u_copy(across, core_peer, 3).start()
        u_arrived(at(z, row_y, 1 - core))
        u_arrived(at(z, 1 - row_y, 1 - core))
        token_block(z)

    def each_side(distance, act):
        pl.when(row_z - distance >= 0)(lambda: act(row_z - distance))
        pl.when(row_z + distance < depth)(lambda: act(row_z + distance))

    each_side(1, relay)
    block_done(row_z)

    def token_step(distance, carry):
        each_side(distance + 1, relay)
        each_side(distance, block_done)
        return carry

    lax.fori_loop(1, depth, token_step, 0)

    parts = []
    for part in range(2):
        mixed = acc_ref[part] * (1.0 / sum_ref[part][:, 0:1])
        mixed = jnp.where(token_heads, mixed, 0.0)
        joined = mixed[0:tokens_dev]
        for head in range(1, half):
            joined = joined + mixed[head * tokens_dev : (head + 1) * tokens_dev]
        parts.append(joined.astype(BF16))
    token_mix = jnp.concatenate(parts, axis=1)
    updated = feat_ref[...] + mm(token_mix, tp_ref[3])
    rowsx_ref[1] = mm(updated.astype(BF16), to_atom_ref[...]).astype(BF16)
    row_sides = block_sides(rowsx_ref.at[1], rowsx_ref, 3)
    start_sides(row_sides)
    place_own = me * atoms_dev + lax.broadcasted_iota(jnp.int32, (atoms_dev, tokens_dev), 0)
    place_own = place_own.astype(F32)

    def returned(block):
        low = rngx_ref[block, 0:1, 0:tokens_dev].astype(F32)
        high = rngx_ref[block, 1:2, 0:tokens_dev].astype(F32)
        member = jnp.where((place_own >= low) & (place_own < high), 1.0, 0.0).astype(BF16)
        return mm(member, rowsx_ref[block])

    gathered = returned(1)
    receive_sides(row_sides)
    x_ref[...] = x_ref[...] + (gathered + returned(0) + returned(2))

    loop_blocks(ENC_LAYERS, ENC_LAYERS + DEC_LAYERS)
    out_ref[0] = x_ref[...].astype(BF16)

    def sent(copy):
        copy.wait_send()

    for copies in (mask_sides, range_sides, enc_sides, row_sides):
        sent_sides(copies)

    def halo_sent(layer, carry):
        sent_sides(halo_sides(layer))
        return carry

    lax.fori_loop(0, ENC_LAYERS + DEC_LAYERS, halo_sent, 0)
    own_sends(sent)
    sent(u_copy(at(row_z, 1 - row_y, core), core_peer, 3))

    def relay_sent(z):
        relay_sends(z, sent)
        sent(u_copy(at(z, 1 - row_y, core), core_peer, 3))

    def sent_step(distance, carry):
        each_side(distance, relay_sent)
        return carry

    lax.fori_loop(1, depth, sent_step, 0)


def shards(
    count,
    atoms,
    s_cond,
    token_start,
    token_len,
    atom_mask,
    atom_bias,
    pair_bias,
    atom_proj,
    atom_up,
    atom_down,
    atom_gains,
    to_token,
    token_proj,
    token_gain,
    to_atom,
):
    atoms_dev, channels = atoms.shape[1:]
    tokens_dev, width = s_cond.shape
    layers = ENC_LAYERS + DEC_LAYERS
    ranges = jnp.stack([token_start, token_start + token_len])
    ranges = jnp.pad(ranges, ((0, 6), (0, -tokens_dev % LANES)))
    mask_rows = atom_mask.reshape(atoms_dev // LANES, LANES)
    vmem = pl.BlockSpec(memory_space=pltpu.VMEM)
    far = pl.BlockSpec(memory_space=pl.ANY)
    half = HT // 2
    return pl.pallas_call(
        functools.partial(kernel, count),
        out_shape=jax.ShapeDtypeStruct(atoms.shape, BF16),
        in_specs=[vmem, vmem, vmem, vmem, far, far] + [vmem] * 5 + [far, vmem, vmem],
        out_specs=vmem,
        scratch_shapes=[
            pltpu.VMEM((atoms_dev, channels), F32),
            pltpu.VMEM((layers, 2, atoms_dev + 2 * RIM, channels), BF16),
            pltpu.VMEM((atoms_dev, channels), BF16),
            pltpu.VMEM((atoms_dev, channels), BF16),
            pltpu.VMEM(atom_bias.shape, F32),
            pltpu.VMEM(pair_bias.shape, BF16),
            pltpu.VMEM(token_proj.shape, BF16),
            pltpu.VMEM((3,) + mask_rows.shape, jnp.int32),
            pltpu.VMEM((atoms_dev // WQ, 1, WK), F32),
            pltpu.VMEM((3,) + ranges.shape, jnp.int32),
            pltpu.VMEM((3, atoms_dev, channels), BF16),
            pltpu.VMEM((3, tokens_dev, channels), BF16),
            pltpu.VMEM((count, tokens_dev, width), BF16),
            pltpu.VMEM((tokens_dev, width), F32),
            pltpu.VMEM((2, half * tokens_dev, width // 2), BF16),
            pltpu.VMEM((2, half * tokens_dev, width // 2), F32),
            pltpu.VMEM((2, half * tokens_dev, LANES), F32),
            pltpu.VMEM((2, half * tokens_dev, LANES), F32),
            pltpu.SemaphoreType.DMA((3,)),
            pltpu.SemaphoreType.DMA((layers, 2)),
            pltpu.SemaphoreType.DMA((layers, 2)),
            pltpu.SemaphoreType.DMA((4, 2)),
            pltpu.SemaphoreType.DMA((4, 2)),
            pltpu.SemaphoreType.DMA((count, 4)),
            pltpu.SemaphoreType.DMA((count,)),
        ],
        compiler_params=pltpu.CompilerParams(
            collective_id=0, has_side_effects=True, vmem_limit_bytes=60 * 1024 * 1024
        ),
    )(
        atoms,
        s_cond,
        ranges,
        mask_rows,
        atom_bias,
        pair_bias,
        atom_proj,
        atom_up,
        atom_down,
        atom_gains,
        to_token,
        token_proj,
        token_gain.reshape(1, width),
        to_atom,
    )


def solution(mesh):
    placed = (
        P("groups", "seq", None),
        P(("groups", "seq"), None),
        P(("groups", "seq")),
        P(("groups", "seq")),
        P(("groups", "seq")),
        P("groups", "seq", None),
        P("groups", "seq", None),
        P(),
        P(),
        P(),
        P(),
        P(),
        P(),
        P(),
        P(),
    )
    return jax.shard_map(
        functools.partial(shards, mesh.shape["seq"]),
        mesh=mesh,
        in_specs=placed,
        out_specs=P("groups", "seq", None),
        check_vma=False,
    )
```

profile of v0, /device:TPU:1, one launch (start us, length us, event | category | flops | bytes accessed | tf_op | source)
XLA Modules:
  0.0 82.6 jit_solution(14803881775639071672)
XLA Ops:
  0.0 0.7 add_bitcast_fusion
  0.7 0.7 pad_add_fusion
  1.3 0.6 pad.4.range_ref
  1.9 1.3 %reshape.7.token_gain_ref = f32[1,768]{1,0:T(1,128)} reshape(f32[768]{0:T(1024)} %param.28) | data formatting | bytes 6144 | tf_op jit(solution)/shard_map/reshape | solution.py:520
  3.2 77.8 %shard_map.145 = bf16[1,512,128]{2,1,0:T(8,128)(2,1)} custom-call(bf16[1,512,128]{2,1,0:T(8,128)(2,1)} %atoms_ref.1, bf16[64,768]{1,0:T(8,128)(2,1)} %s_cond_ref.1, s32[8,128]{1,0:T(8,128)} %pad.4.range_ref, s32[4,128]{1,0:T(4,128)} %bitcast.4, f32[4,512,128]{2,1,0:T(8,128)} %bias_hbm.1, bf16[16,64,1024]{2,1,0:T(8,128)(2,1)} %pair_hbm.1, ...), custom_call_target="tpu_custom_call" | custom-call | tf_op jit(solution)/shard_map/pallas_call | solution.py:472
  81.0 1.6 %copy.17 = bf16[1,512,128]{2,1,0:T(8,128)(2,1)} copy(bf16[1,512,128]{2,1,0:T(8,128)(2,1)} %shard_map.145) | data formatting | bytes 262144
where the time goes:
time: 82.8 us; the launch traced here: 82.6 us
  Pallas kernels  77.8 us (94%)
  local copies, waits for them, and re-layouts  3.44 us (4%)
  other arithmetic  1.34 us (2%)
    pallas_call x1, Pallas kernels, shards(): pl.pallas_call(functools.partial(kernel, count), out_shape=jax.ShapeDtype...  77.8 us

commit v1 on v0

--- a/solution.py
+++ b/solution.py
@@ -50,7 +50,8 @@
     count,
     atoms_ref,
     s_cond_ref,
-    range_ref,
+    start_ref,
+    length_ref,
     mask_ref,
     bias_hbm,
     pair_hbm,
@@ -80,7 +81,6 @@
     qbd_ref,
     acc_ref,
     max_ref,
-    sum_ref,
     load_sem,
     halo_send,
     halo_recv,
@@ -124,8 +124,10 @@
     pair_load.start()
 
     x_ref[...] = atoms_ref[0].astype(F32)
-    mex_ref[1] = mask_ref[...]
-    rngx_ref[1] = range_ref[...]
+    mex_ref[1] = mask_ref[...].reshape(mex_ref.shape[1:])
+    starts = start_ref[...].reshape(1, tokens_dev)
+    rngx_ref[1, 0:1, 0:tokens_dev] = starts
+    rngx_ref[1, 1:2, 0:tokens_dev] = starts + length_ref[...].reshape(1, tokens_dev)
 
     def clear(slot, edge):
         for ref in (mex_ref, rngx_ref, encx_ref, rowsx_ref):
@@ -184,8 +186,8 @@
             lambda side: halo_recv.at[layer, side],
         )
 
-    mask_sides = block_sides(mask_ref, mex_ref, 0)
-    range_sides = block_sides(range_ref, rngx_ref, 1)
+    mask_sides = block_sides(mex_ref.at[1], mex_ref, 0)
+    range_sides = block_sides(rngx_ref.at[1], rngx_ref, 1)
     start_sides(mask_sides)
     start_sides(range_sides)
 
@@ -215,13 +217,14 @@
             atom_heads, jnp.concatenate([query] * HA, axis=0), jnp.zeros((), BF16)
         )
         keys = kv_ref[layer, 0, pl.ds(first, WK), :]
-        values = kv_ref[layer, 1, pl.ds(first, WK), :]
+        values = jnp.concatenate(
+            [kv_ref[layer, 1, pl.ds(first, WK), :], jnp.ones((WK, channels), BF16)], axis=1
+        )
         bias = bias_ref[:, pl.ds(first, WQ), :].reshape(HA * WQ, WK)
         logits = mm_nt(tall, keys) * head_size ** (-0.5) + bias + wmask_ref[window]
         weights = jnp.exp(logits - jnp.max(logits, axis=-1, keepdims=True))
-        total = jnp.sum(weights, axis=-1, keepdims=True)
-        mixed = mm(weights.astype(BF16), values) * (1.0 / total)
-        mixed = jnp.where(atom_heads, mixed, 0.0)
+        both = mm(weights.astype(BF16), values)
+        mixed = jnp.where(atom_heads, both[:, :channels] / both[:, channels:], 0.0)
         joined = mixed[0:WQ]
         for head in range(1, HA):
             joined = joined + mixed[head * WQ : (head + 1) * WQ]
@@ -294,7 +297,7 @@
     totals = totals + pooled(0) + pooled(2)
     features = totals / (end_col - start_col) + s_cond_ref[...].astype(F32)
     feat_ref[...] = features
-    uall_ref[me] = layer_norm(features, token_gain_ref[...]).astype(BF16)
+    uall_ref[me] = layer_norm(features, token_gain_ref[...].reshape(1, width)).astype(BF16)
 
     def at(z, y, c):
         return (z * 2 + y) * 2 + c
@@ -342,7 +345,6 @@
             token_heads, jnp.concatenate([query] * half, axis=0), jnp.zeros((), BF16)
         )
     max_ref[...] = jnp.full_like(max_ref, -1e30)
-    sum_ref[...] = jnp.zeros_like(sum_ref)
     acc_ref[...] = jnp.zeros_like(acc_ref)
     pair_load.wait()
     span = 4 * tokens_dev
@@ -354,6 +356,7 @@
             cols = slice(part * half_width, (part + 1) * half_width)
             keys = mm(rows, tp_ref[1, :, cols]).astype(BF16)
             values = mm(rows, tp_ref[2, :, cols]).astype(BF16)
+            values = jnp.concatenate([values, jnp.ones((span, LANES), BF16)], axis=1)
             bias = pair_ref[part * half : (part + 1) * half, :, pl.ds(first, span)]
             bias = bias.reshape(half * tokens_dev, span).astype(F32)
             logits = mm_nt(qbd_ref[part], keys) * token_head ** (-0.5) + bias
@@ -361,10 +364,8 @@
             now = jnp.maximum(before, jnp.max(logits, axis=-1, keepdims=True))
             weights = jnp.exp(logits - now)
             shrink = jnp.exp(before - now)
-            total = sum_ref[part][:, 0:1] * shrink + jnp.sum(weights, axis=-1, keepdims=True)
             acc_ref[part] = acc_ref[part] * shrink + mm(weights.astype(BF16), values)
             max_ref[part] = jnp.broadcast_to(now, max_ref.shape[1:])
-            sum_ref[part] = jnp.broadcast_to(total, sum_ref.shape[1:])
 
     def block_done(z):
         across = at(z, 1 - row_y, core)
@@ -390,7 +391,7 @@
 
     parts = []
     for part in range(2):
-        mixed = acc_ref[part] * (1.0 / sum_ref[part][:, 0:1])
+        mixed = acc_ref[part, :, 0:half_width] * (1.0 / acc_ref[part, :, half_width : half_width + 1])
         mixed = jnp.where(token_heads, mixed, 0.0)
         joined = mixed[0:tokens_dev]
         for head in range(1, half):
@@ -463,16 +464,13 @@
     atoms_dev, channels = atoms.shape[1:]
     tokens_dev, width = s_cond.shape
     layers = ENC_LAYERS + DEC_LAYERS
-    ranges = jnp.stack([token_start, token_start + token_len])
-    ranges = jnp.pad(ranges, ((0, 6), (0, -tokens_dev % LANES)))
-    mask_rows = atom_mask.reshape(atoms_dev // LANES, LANES)
     vmem = pl.BlockSpec(memory_space=pltpu.VMEM)
     far = pl.BlockSpec(memory_space=pl.ANY)
     half = HT // 2
     return pl.pallas_call(
         functools.partial(kernel, count),
         out_shape=jax.ShapeDtypeStruct(atoms.shape, BF16),
-        in_specs=[vmem, vmem, vmem, vmem, far, far] + [vmem] * 5 + [far, vmem, vmem],
+        in_specs=[vmem] * 5 + [far, far] + [vmem] * 5 + [far, vmem, vmem],
         out_specs=vmem,
         scratch_shapes=[
             pltpu.VMEM((atoms_dev, channels), F32),
@@ -482,16 +480,15 @@
             pltpu.VMEM(atom_bias.shape, F32),
             pltpu.VMEM(pair_bias.shape, BF16),
             pltpu.VMEM(token_proj.shape, BF16),
-            pltpu.VMEM((3,) + mask_rows.shape, jnp.int32),
+            pltpu.VMEM((3, atoms_dev // LANES, LANES), jnp.int32),
             pltpu.VMEM((atoms_dev // WQ, 1, WK), F32),
-            pltpu.VMEM((3,) + ranges.shape, jnp.int32),
+            pltpu.VMEM((3, 8, pl.cdiv(tokens_dev, LANES) * LANES), jnp.int32),
             pltpu.VMEM((3, atoms_dev, channels), BF16),
             pltpu.VMEM((3, tokens_dev, channels), BF16),
             pltpu.VMEM((count, tokens_dev, width), BF16),
             pltpu.VMEM((tokens_dev, width), F32),
             pltpu.VMEM((2, half * tokens_dev, width // 2), BF16),
-            pltpu.VMEM((2, half * tokens_dev, width // 2), F32),
-            pltpu.VMEM((2, half * tokens_dev, LANES), F32),
+            pltpu.VMEM((2, half * tokens_dev, width // 2 + LANES), F32),
             pltpu.VMEM((2, half * tokens_dev, LANES), F32),
             pltpu.SemaphoreType.DMA((3,)),
             pltpu.SemaphoreType.DMA((layers, 2)),
@@ -507,8 +504,9 @@
     )(
         atoms,
         s_cond,
-        ranges,
-        mask_rows,
+        token_start,
+        token_len,
+        atom_mask,
         atom_bias,
         pair_bias,
         atom_proj,
@@ -517,7 +515,7 @@
         atom_gains,
         to_token,
         token_proj,
-        token_gain.reshape(1, width),
+        token_gain,
         to_atom,
     )
 

time: 82.8 us -> 74.4 us (0.90)
  Pallas kernels: 77.8 us -> 72.7 us
  local copies, waits for them, and re-layouts: 3.44 us -> 1.57 us
  other arithmetic: 1.34 us -> 0 us
    pallas_call x1, Pallas kernels: 77.8 us -> 72.7 us  [shards(): pl.pallas_call(functools.partial(kernel, count), out_shape=jax.ShapeDtype...]
    another operation x2 -> x0, other arithmetic: 1.34 us -> none  [shards(): ranges = jnp.stack([token_start, token_start + token_len])]
    reshape x1 -> x0, local copies, waits for them, and re-layouts: 1.27 us -> none  [shards(): token_gain.reshape(1, width)]
where the time goes in v1:
time: 74.4 us; the launch traced here: 74.2 us
  Pallas kernels  72.7 us (98%)
  local copies, waits for them, and re-layouts  1.57 us (2%)
    pallas_call x1, Pallas kernels, shards(): pl.pallas_call(functools.partial(kernel, count), out_shape=jax.ShapeDtype...  72.7 us
    unnamed x1, local copies, waits for them, and re-layouts  1.57 us

profile of v1, /device:TPU:1, one launch (start us, length us, event | category | flops | bytes accessed | tf_op | source)
XLA Modules:
  0.0 74.2 jit_solution(13815687097611853562)
XLA Ops:
  0.0 72.7 %shard_map.145 = bf16[1,512,128]{2,1,0:T(8,128)(2,1)} custom-call(bf16[1,512,128]{2,1,0:T(8,128)(2,1)} %atoms_ref.1, bf16[64,768]{1,0:T(8,128)(2,1)} %s_cond_ref.1, s32[64]{0:T(128)} %start_ref.1, s32[64]{0:T(128)} %length_ref.1, s32[512]{0:T(512)} %mask_ref.1, f32[4,512,128]{2,1,0:T(8,128)} %bias_hbm.1, bf16[16,64,1024]{2,1,0:T(8,128)(2,1)} %pair_hbm.1, ...), custom_call_target="tpu_custom_call" | custom-call | tf_op jit(solution)/shard_map/pallas_call | solution.py:470
  72.7 1.6 %copy.17 = bf16[1,512,128]{2,1,0:T(8,128)(2,1)} copy(bf16[1,512,128]{2,1,0:T(8,128)(2,1)} %shard_map.145) | data formatting | bytes 262144

commit v2 on v1

--- a/solution.py
+++ b/solution.py
@@ -14,8 +14,7 @@
 ENC_LAYERS = 3
 DEC_LAYERS = 3
 RIM = (WK - WQ) // 2
-GROUP = 4
-CHUNK = 256
+CHUNK = 512
 LANES = 128
 
 epsilon = 1e-05
@@ -211,7 +210,7 @@
     atom_heads = head_mask(HA * WQ, WQ, channels, head_size)
 
     def attend(layer, window):
-        first = pl.multiple_of(window * WQ, WQ)
+        first = window * WQ
         query = q_ref[pl.ds(first, WQ), :]
         tall = jnp.where(
             atom_heads, jnp.concatenate([query] * HA, axis=0), jnp.zeros((), BF16)
@@ -242,12 +241,8 @@
             q_ref[base : base + CHUNK] = mm(normed, proj_ref[layer, 0]).astype(BF16)
         start_sides(copies)
 
-        def inner(step, carry):
-            for part in range(GROUP):
-                attend(layer, 2 + step * GROUP + part)
-            return carry
-
-        lax.fori_loop(0, (windows - 4) // GROUP, inner, 0)
+        for window in range(2, windows - 2):
+            attend(layer, window)
         receive_sides(copies)
         for window in (0, 1, windows - 2, windows - 1):
             attend(layer, window)

time: 74.4 us -> 66.9 us (0.90)
  Pallas kernels: 72.7 us -> 64.6 us
    pallas_call x1, Pallas kernels: 72.7 us -> 64.6 us  [shards(): pl.pallas_call(functools.partial(kernel, count), out_shape=jax.ShapeDtype...]
where the time goes in v2:
time: 66.9 us; the launch traced here: 66.2 us
  Pallas kernels  64.6 us (97%)
  local copies, waits for them, and re-layouts  1.57 us (2%)
    pallas_call x1, Pallas kernels, shards(): pl.pallas_call(functools.partial(kernel, count), out_shape=jax.ShapeDtype...  64.6 us
    unnamed x1, local copies, waits for them, and re-layouts  1.57 us

profile of v2, /device:TPU:1, one launch (start us, length us, event | category | flops | bytes accessed | tf_op | source)
XLA Modules:
  0.0 66.2 jit_solution(13074073556210964950)
XLA Ops:
  0.0 64.6 %shard_map.145 = bf16[1,512,128]{2,1,0:T(8,128)(2,1)} custom-call(bf16[1,512,128]{2,1,0:T(8,128)(2,1)} %atoms_ref.1, bf16[64,768]{1,0:T(8,128)(2,1)} %s_cond_ref.1, s32[64]{0:T(128)} %start_ref.1, s32[64]{0:T(128)} %length_ref.1, s32[512]{0:T(512)} %mask_ref.1, f32[4,512,128]{2,1,0:T(8,128)} %bias_hbm.1, bf16[16,64,1024]{2,1,0:T(8,128)(2,1)} %pair_hbm.1, ...), custom_call_target="tpu_custom_call" | custom-call | tf_op jit(solution)/shard_map/pallas_call | solution.py:465
  64.6 1.6 %copy.17 = bf16[1,512,128]{2,1,0:T(8,128)(2,1)} copy(bf16[1,512,128]{2,1,0:T(8,128)(2,1)} %shard_map.145) | data formatting | bytes 262144

commit v3 on v2

--- a/solution.py
+++ b/solution.py
@@ -14,7 +14,6 @@
 ENC_LAYERS = 3
 DEC_LAYERS = 3
 RIM = (WK - WQ) // 2
-CHUNK = 512
 LANES = 128
 
 epsilon = 1e-05
@@ -232,28 +231,37 @@
     def atom_block(layer):
         copies = halo_sides(layer)
         gain = gains_ref[layer]
-        for base in range(0, atoms_dev, CHUNK):
-            normed = layer_norm(x_ref[base : base + CHUNK], gain[0:1]).astype(BF16)
-            for kind in range(2):
-                kv_ref[layer, kind, RIM + base : RIM + base + CHUNK] = mm(
-                    normed, proj_ref[layer, kind + 1]
-                ).astype(BF16)
-            q_ref[base : base + CHUNK] = mm(normed, proj_ref[layer, 0]).astype(BF16)
+        normed = layer_norm(x_ref[...], gain[0:1]).astype(BF16)
+        for kind in range(2):
+            kv_ref[layer, kind, RIM : RIM + atoms_dev] = mm(
+                normed, proj_ref[layer, kind + 1]
+            ).astype(BF16)
         start_sides(copies)
+        q_ref[...] = mm(normed, proj_ref[layer, 0]).astype(BF16)
 
         for window in range(2, windows - 2):
             attend(layer, window)
         receive_sides(copies)
         for window in (0, 1, windows - 2, windows - 1):
             attend(layer, window)
-        for base in range(0, atoms_dev, CHUNK):
-            stream = x_ref[base : base + CHUNK] + mm(
-                mix_ref[base : base + CHUNK], proj_ref[layer, 3]
-            )
+
+        def transition(rows, mixture):
+            stream = rows + mm(mixture, proj_ref[layer, 3])
             second = layer_norm(stream, gain[1:2]).astype(BF16)
             gated = jax.nn.silu(mm(second, up_ref[layer, 0]))
             hidden = (gated * mm(second, up_ref[layer, 1])).astype(BF16)
-            x_ref[base : base + CHUNK] = stream + mm(hidden, down_ref[layer])
+            return stream + mm(hidden, down_ref[layer])
+
+        rim = 2 * WQ
+        inside = slice(rim, atoms_dev - rim)
+        x_ref[inside] = transition(x_ref[inside], mix_ref[inside])
+
+        def ends(ref):
+            return jnp.concatenate([ref[0:rim], ref[atoms_dev - rim : atoms_dev]], axis=0)
+
+        outer = transition(ends(x_ref), ends(mix_ref))
+        x_ref[0:rim] = outer[0:rim]
+        x_ref[atoms_dev - rim : atoms_dev] = outer[rim:]
 
     def loop_blocks(low, high):
         def step(layer, carry):

time: 66.9 us -> 67.4 us (level)
  no operation moved by 1% of the time
where the time goes in v3:
time: 67.4 us; the launch traced here: 66.7 us
  Pallas kernels  65.1 us (97%)
  local copies, waits for them, and re-layouts  1.57 us (2%)
    pallas_call x1, Pallas kernels, shards(): pl.pallas_call(functools.partial(kernel, count), out_shape=jax.ShapeDtype...  65.1 us
    unnamed x1, local copies, waits for them, and re-layouts  1.57 us

profile of v3, /device:TPU:1, one launch (start us, length us, event | category | flops | bytes accessed | tf_op | source)
XLA Modules:
  0.0 66.7 jit_solution(7235816090139787135)
XLA Ops:
  0.0 65.1 %shard_map.145 = bf16[1,512,128]{2,1,0:T(8,128)(2,1)} custom-call(bf16[1,512,128]{2,1,0:T(8,128)(2,1)} %atoms_ref.1, bf16[64,768]{1,0:T(8,128)(2,1)} %s_cond_ref.1, s32[64]{0:T(128)} %start_ref.1, s32[64]{0:T(128)} %length_ref.1, s32[512]{0:T(512)} %mask_ref.1, f32[4,512,128]{2,1,0:T(8,128)} %bias_hbm.1, bf16[16,64,1024]{2,1,0:T(8,128)(2,1)} %pair_hbm.1, ...), custom_call_target="tpu_custom_call" | custom-call | tf_op jit(solution)/shard_map/pallas_call | solution.py:473
  65.1 1.6 %copy.17 = bf16[1,512,128]{2,1,0:T(8,128)(2,1)} copy(bf16[1,512,128]{2,1,0:T(8,128)(2,1)} %shard_map.145) | data formatting | bytes 262144
